TPU v7x, 256 devices: a whole 4x4x8 slice. The times are simulated.
256 devices in a mesh: slab: 32 (over z, y), snap: 8 (over x, core).
Axes of the slice: x: 4, y: 4, z: 8, core: 2. Of those that a mesh axis runs over, the one named last changes fastest.
Arguments:
- flow: bfloat16 [128, 3, 64, 64, 128], P('snap', None, 'slab'), may hold values from -127 to 127
- large_scale: bfloat16 [3, 64, 64, 128], P(None, 'slab'), may hold values from -6 to 6
- modulation: float32 [128, 64], replicated, may hold values from -15 to 15
- metric: float32 [4, 64, 64, 128], P(None, 'slab'), may hold values from -0.5 to 9.6
Outputs:
- whitened: float32 [128, 3, 64, 64, 128], P(None, None, 'slab', 'snap')
All inputs are finite; a program needn't handle non-finite values.
Results may differ from a plain program's by a relative error of at most 0.0003.
Values may be sent and summed in bfloat16 or wider, within the bound.
A program may use at most 64 MiB of HBM per device.

v0:
```python
import jax
import jax.numpy as jnp
from jax import lax
from jax.sharding import PartitionSpec as P

NSITER = 6


def with_halo(block, sides, width):
    for axis, dim in sides:
        count = lax.axis_size(axis)
        forward = [(i, i + 1) for i in range(count - 1)]
        backward = [(target, source) for source, target in forward]
        low = lax.ppermute(
            lax.slice_in_dim(block, block.shape[dim] - width, None, axis=dim), axis, forward
        )
        high = lax.ppermute(lax.slice_in_dim(block, 0, width, axis=dim), axis, backward)
        block = jnp.concatenate([low, block, high], axis=dim)
    return block


def vorticity(velocity, metric):
    metric_x = metric[0]
    shear_xy = metric[1]
    metric_y = metric[2]
    metric_z = metric[3]

    def along_x(values):
        return 0.5 * (values[..., 1:-1, 2:, :] - values[..., 1:-1, :-2, :])

    def along_y(values):
        return 0.5 * (values[..., 2:, 1:-1, :] - values[..., :-2, 1:-1, :])

    def along_z(values):
        center = values[..., 1:-1, 1:-1, :]
        return 0.5 * (jnp.roll(center, -1, -1) - jnp.roll(center, 1, -1))

    def slope_x(values):
        return metric_x * along_x(values) + shear_xy * along_y(values)

    def slope_y(values):
        return metric_y * along_y(values)

    def slope_z(values):
        return metric_z * along_z(values)

    stream = velocity[..., 0, :, :, :]
    normal = velocity[..., 1, :, :, :]
    spanwise = velocity[..., 2, :, :, :]
    around_x = slope_y(spanwise) - slope_z(normal)
    around_y = slope_z(stream) - slope_x(spanwise)
    around_z = slope_x(normal) - slope_y(stream)
    return jnp.stack([around_x, around_y, around_z], axis=-4)


def wrap_columns(values):
    return jnp.concatenate([values[..., -1:, :], values, values[..., :1, :]], axis=-2)


def whitening(correlation):
    identity = jnp.eye(correlation.shape[0], dtype=correlation.dtype)
    frob_scale = jnp.sqrt(jnp.sum(correlation * correlation) + 1e-06)
    approx = correlation / frob_scale
    inverse = identity
    for repeat in range(NSITER):
        factor = 0.5 * (3.0 * identity - jnp.dot(inverse, approx, precision=lax.Precision.HIGHEST))
        approx = jnp.dot(approx, factor, precision=lax.Precision.HIGHEST)
        inverse = jnp.dot(factor, inverse, precision=lax.Precision.HIGHEST)
    return inverse / jnp.sqrt(frob_scale)


def inner_rows(left_rows, right_rows):
    return lax.dot_general(
        left_rows,
        right_rows,
        (((1,), (1,)), ((), ())),
        precision=lax.Precision.HIGHEST,
        preferred_element_type=jnp.float32,
    )


def planes_padded(flow, large_scale):
    joined = jnp.concatenate([flow, large_scale[None]], axis=0)
    return with_halo(joined, (("slab", 2),), 1)


def per_device(flow, large_scale, modulation, metric):
    snap_count = lax.axis_size("snap")
    slab_count = lax.axis_size("slab")
    own_snaps = flow.shape[0]
    block_cols = flow.shape[3] // snap_count
    snap_index = lax.axis_index("snap")
    mod_ext = jnp.concatenate([modulation[:, -1:], modulation, modulation[:, :1]], axis=1)
    padded = planes_padded(flow, large_scale)
    large_ext = wrap_columns(padded[own_snaps].astype(jnp.float32))
    mod_mine = lax.dynamic_slice_in_dim(mod_ext, snap_index * own_snaps, own_snaps, 0)
    velocity = (
        wrap_columns(padded[:own_snaps].astype(jnp.float32))
        + mod_mine[:, None, None, :, None] * large_ext[None]
    )
    local_fields = vorticity(velocity, metric)
    pieces = local_fields.reshape(
        own_snaps, 3, local_fields.shape[2], snap_count, block_cols, local_fields.shape[4]
    )
    fields = lax.all_to_all(pieces, "snap", split_axis=3, concat_axis=0, tiled=True)[:, :, :, 0]
    snapshot_rows = fields.reshape(fields.shape[0], -1)
    gram_local = inner_rows(snapshot_rows, snapshot_rows)
    gram_total = lax.psum(gram_local, ("slab", "snap"))
    correlation = gram_total / (snapshot_rows.shape[1] * slab_count * snap_count)
    weights = whitening(correlation)
    result = jnp.dot(weights, snapshot_rows, precision=lax.Precision.HIGHEST)
    return result.reshape(fields.shape)


def solution(mesh):
    return jax.shard_map(
        per_device,
        mesh=mesh,
        in_specs=(
            P("snap", None, "slab", None, None),
            P(None, "slab", None, None),
            P(),
            P(None, "slab", None, None),
        ),
        out_specs=P(None, None, "slab", "snap", None),
        check_vma=False,
    )
```

profile of v0, /device:TPU:1, one launch (start us, length us, event | category | flops | bytes accessed | tf_op | source)
XLA Modules:
  0.0 358.1 jit_solution(2387422955889473556)
XLA Ops:
  6.5 2.9 fusion.21
  9.4 4.1 %collective-permute-start = (bf16[17,3,1,64,128]{4,3,2,1,0:T(8,128)(2,1)}, bf16[17,3,1,64,128]{4,3,2,1,0:T(8,128)(2,1)S(1)}, u32[]{:S(2)}, u32[]{:S(2)}) collective-permute-start(bf16[17,3,1,64,128]{4,3,2,1,0:T(8,128)(2,1)} %get-tuple-element.20), channel_id=1, source_target_pairs={{0,8},{8,16},{16,24},{24,32},{32,40},{40,48},{48,56},{56,64},{64,7... | collective-permute-start | bytes 2506760 | tf_op jit(solution)/shard_map/ppermute | solution.py:14
  13.5 1.3 collective-permute-start.1
  15.0 1.0 multiply_bitcast_fusion.2
  15.9 15.1 %collective-permute-done = bf16[17,3,1,64,128]{4,3,2,1,0:T(8,128)(2,1)S(1)} collective-permute-done((bf16[17,3,1,64,128]{4,3,2,1,0:T(8,128)(2,1)}, bf16[17,3,1,64,128]{4,3,2,1,0:T(8,128)(2,1)S(1)}, u32[]{:S(2)}, u32[]{:S(2)}) %collective-permute-start) | collective-permute-done | bytes 835616 | tf_op jit(solution)/shard_map/ppermute | solution.py:14
  31.0 3.8 %collective-permute-done.1 = bf16[17,3,1,64,128]{4,3,2,1,0:T(8,128)(2,1)S(1)} collective-permute-done((bf16[17,3,1,64,128]{4,3,2,1,0:T(8,128)(2,1)}, bf16[17,3,1,64,128]{4,3,2,1,0:T(8,128)(2,1)S(1)}, u32[]{:S(2)}, u32[]{:S(2)}) %collective-permute-start.1) | collective-permute-done | bytes 835616 | tf_op jit(solution)/shard_map/ppermute | solution.py:17
  34.8 0.5 pad_maximum_fusion
  35.3 0.7 slice_convert_fusion
  36.3 1.5 maximum_add_fusion
  37.7 0.5 slice_bitcast_fusion.2
  38.2 0.9 fusion.28
  39.1 0.9 fusion.29
  40.0 0.8 fusion.9
  40.7 1.5 fusion.19
  42.2 0.2 pad_maximum_fusion.1
  42.5 0.3 copy.19
  42.8 43.4 %all_to_all.15 = f32[16,3,2,8,8,128]{5,4,2,1,0,3:T(8,128)} all-to-all(f32[16,3,2,8,8,128]{5,4,2,1,0,3:T(8,128)S(1)} %copy.19), channel_id=1, replica_groups=mesh['slab'=32,'snap'=8] {'snap'}, dimensions={3} | all-to-all | bytes 6291456 | tf_op jit(solution)/shard_map/all_to_all | solution.py:105
  86.2 2.8 reshape_squeeze.3
  89.0 3.2 fusion.34
  92.2 2.4 copy.16
  94.6 242.7 %all-reduce.2.cloned.1.call-done = f32[128,128]{1,0:T(8,128)} async-done(((f32[128,128]{1,0:T(8,128)}), f32[128,128]{1,0:T(8,128)}) %all-reduce.2.cloned.1.call-update) | async-done | bytes 65552 | tf_op jit(solution)/shard_map/psum | solution.py:108
  337.3 1.5 multiply_reduce_fusion
  339.5 1.0 fusion.6
  340.7 1.0 fusion.24
  341.8 0.2 fusion.5
  342.4 0.2 fusion.4
  343.0 0.2 fusion.3
  343.7 0.2 fusion.2
  344.3 0.2 fusion.1
  344.5 0.2 fusion
  344.7 3.0 fusion.43
  347.8 3.5 copy.17
  (26 shorter events, 2.2 us)
Async XLA Ops:
  6.5 28.2 %copy-start = (bf16[16,3,2,64,128]{4,3,2,1,0:T(8,128)(2,1)S(1)}, bf16[16,3,2,64,128]{4,3,2,1,0:T(8,128)(2,1)}, u32[]{:S(2)}) copy-start(bf16[16,3,2,64,128]{4,3,2,1,0:T(8,128)(2,1)} %param.4) | copy-start | bytes 4718596
  6.5 28.2 %copy-start.2 = (bf16[3,2,64,128]{3,2,1,0:T(8,128)(2,1)S(1)}, bf16[3,2,64,128]{3,2,1,0:T(8,128)(2,1)}, u32[]{:S(2)}) copy-start(bf16[3,2,64,128]{3,2,1,0:T(8,128)(2,1)} %param.5) | copy-start | bytes 294916
  6.5 8.2 %copy-start.3 = (f32[128,64]{0,1:T(8,128)S(1)}, f32[128,64]{0,1:T(8,128)}, u32[]{:S(2)}) copy-start(f32[128,64]{0,1:T(8,128)} %param.6) | copy-start | bytes 98308
  6.5 330.8 %all-reduce.2.cloned.1.call-start = ((), (), s32[]{:S(2)}) async-start(), calls=%async_computation.1 | async-start | bytes 131072 | tf_op jit(solution)/shard_map/psum | solution.py:108
  9.4 21.6 %collective-permute-start = (bf16[17,3,1,64,128]{4,3,2,1,0:T(8,128)(2,1)}, bf16[17,3,1,64,128]{4,3,2,1,0:T(8,128)(2,1)S(1)}, u32[]{:S(2)}, u32[]{:S(2)}) collective-permute-start(bf16[17,3,1,64,128]{4,3,2,1,0:T(8,128)(2,1)} %get-tuple-element.20), channel_id=1, source_target_pairs={{0,8},{8,16},{16,24},{24,32},{32,40},{40,48},{48,56},{56,64},{64,7... | collective-permute-start | bytes 2506760 | tf_op jit(solution)/shard_map/ppermute | solution.py:14
  13.5 21.3 %collective-permute-start.1 = (bf16[17,3,1,64,128]{4,3,2,1,0:T(8,128)(2,1)}, bf16[17,3,1,64,128]{4,3,2,1,0:T(8,128)(2,1)S(1)}, u32[]{:S(2)}, u32[]{:S(2)}) collective-permute-start(bf16[17,3,1,64,128]{4,3,2,1,0:T(8,128)(2,1)} %get-tuple-element.21), channel_id=1, source_target_pairs={{8,0},{16,8},{24,16},{32,24},{40,32},{48,40},{56,48},{64,56},{72,6... | collective-permute-start | bytes 2506760 | tf_op jit(solution)/shard_map/ppermute | solution.py:17
  94.6 250.2 %copy-start.1 = (f32[6144,128]{1,0:T(8,128)S(1)}, f32[6144,128]{1,0:T(8,128)}, u32[]{:S(2)}) copy-start(f32[6144,128]{1,0:T(8,128)} %copy.16) | copy-start | bytes 9437188
Sparse Core Ops, SparseCore 0:
  92.3 244.9 all-reduce.1
where the time goes:
time: 358 us
  waiting for transfers between devices  262 us (73%)
  blocking collectives  43.4 us (12%)
  between operations  14.4 us (4%)
  local copies, waits for them, and re-layouts  11.3 us (3%)
  matrix products  11.3 us (3%)
  other arithmetic  10.6 us (3%)
  starting transfers between devices  5.35 us (1%)
    psum x1, waiting for transfers between devices, per_device(): gram_total = lax.psum(gram_local, ('slab', 'snap'))  243 us
    all_to_all x1, blocking collectives, per_device(): lax.all_to_all(pieces, 'snap', split_axis=3, concat_axis=0, tiled=True)  43.4 us
    ppermute x1, waiting for transfers between devices, with_halo(): lax.ppermute(lax.slice_in_dim(block, block.shape[dim] - width, None, axis...  15.1 us
  transfers between devices with their start and end apart: 3, of which 3 were waited for; matrix products, arithmetic and copies ran while one was open for 1% of the time, Pallas kernels for 0%

commit v1 on v0

--- a/solution.py
+++ b/solution.py
@@ -105,7 +105,7 @@
     fields = lax.all_to_all(pieces, "snap", split_axis=3, concat_axis=0, tiled=True)[:, :, :, 0]
     snapshot_rows = fields.reshape(fields.shape[0], -1)
     gram_local = inner_rows(snapshot_rows, snapshot_rows)
-    gram_total = lax.psum(gram_local, ("slab", "snap"))
+    gram_total = lax.psum(lax.psum(gram_local, axis_name="slab"), axis_name="snap")
     correlation = gram_total / (snapshot_rows.shape[1] * slab_count * snap_count)
     weights = whitening(correlation)
     result = jnp.dot(weights, snapshot_rows, precision=lax.Precision.HIGHEST)

time: 358 us -> 323 us (0.902)
  waiting for transfers between devices: 262 us -> 224 us
    psum x1 -> x2, waiting for transfers between devices: 243 us -> 205 us  [the longest x1 140 us: per_device(): lax.psum(gram_local, axis_name='slab')]
  transfers between devices with their start and end apart: 3 -> 4, of which waited for: 3 -> 4; matrix products, arithmetic and copies ran while one was open for 1% -> 1% of each run, Pallas kernels for 0% -> 0%
where the time goes in v1:
time: 323 us; the launch traced here: 321 us
  waiting for transfers between devices  224 us (69%)
  blocking collectives  43.4 us (13%)
  between operations  14.4 us (4%)
  local copies, waits for them, and re-layouts  11.3 us (3%)
  matrix products  11.3 us (3%)
  other arithmetic  10.6 us (3%)
  starting transfers between devices  5.58 us (2%)
    psum x1, waiting for transfers between devices, per_device(): lax.psum(gram_local, axis_name='slab')  140 us
    psum x1, waiting for transfers between devices, per_device(): lax.psum(lax.psum(gram_local, axis_name='slab'), axis_name='snap')  65.2 us
    all_to_all x1, blocking collectives, per_device(): lax.all_to_all(pieces, 'snap', split_axis=3, concat_axis=0, tiled=True)  43.4 us
    ppermute x1, waiting for transfers between devices, with_halo(): lax.ppermute(lax.slice_in_dim(block, block.shape[dim] - width, None, axis...  15.1 us
  transfers between devices with their start and end apart: 4, of which 4 were waited for; matrix products, arithmetic and copies ran while one was open for 1% of the time, Pallas kernels for 0%

profile of v1, /device:TPU:1, one launch (start us, length us, event | category | flops | bytes accessed | tf_op | source)
XLA Modules:
  0.0 321.0 jit_solution(16249024335755964417)
XLA Ops:
  6.5 2.9 fusion.21
  9.4 4.1 %collective-permute-start = (bf16[17,3,1,64,128]{4,3,2,1,0:T(8,128)(2,1)}, bf16[17,3,1,64,128]{4,3,2,1,0:T(8,128)(2,1)S(1)}, u32[]{:S(2)}, u32[]{:S(2)}) collective-permute-start(bf16[17,3,1,64,128]{4,3,2,1,0:T(8,128)(2,1)} %get-tuple-element.20), channel_id=1, source_target_pairs={{0,8},{8,16},{16,24},{24,32},{32,40},{40,48},{48,56},{56,64},{64,7... | collective-permute-start | bytes 2506760 | tf_op jit(solution)/shard_map/ppermute | solution.py:14
  13.5 1.3 collective-permute-start.1
  15.0 1.0 multiply_bitcast_fusion.2
  15.9 15.1 %collective-permute-done = bf16[17,3,1,64,128]{4,3,2,1,0:T(8,128)(2,1)S(1)} collective-permute-done((bf16[17,3,1,64,128]{4,3,2,1,0:T(8,128)(2,1)}, bf16[17,3,1,64,128]{4,3,2,1,0:T(8,128)(2,1)S(1)}, u32[]{:S(2)}, u32[]{:S(2)}) %collective-permute-start) | collective-permute-done | bytes 835616 | tf_op jit(solution)/shard_map/ppermute | solution.py:14
  31.0 3.8 %collective-permute-done.1 = bf16[17,3,1,64,128]{4,3,2,1,0:T(8,128)(2,1)S(1)} collective-permute-done((bf16[17,3,1,64,128]{4,3,2,1,0:T(8,128)(2,1)}, bf16[17,3,1,64,128]{4,3,2,1,0:T(8,128)(2,1)S(1)}, u32[]{:S(2)}, u32[]{:S(2)}) %collective-permute-start.1) | collective-permute-done | bytes 835616 | tf_op jit(solution)/shard_map/ppermute | solution.py:17
  34.8 0.5 pad_maximum_fusion
  35.3 0.7 slice_convert_fusion
  36.3 1.5 maximum_add_fusion
  37.7 0.5 slice_bitcast_fusion.2
  38.2 0.9 fusion.28
  39.1 0.9 fusion.29
  40.0 0.8 fusion.9
  40.7 1.5 fusion.19
  42.2 0.2 pad_maximum_fusion.1
  42.5 0.3 copy.19
  42.8 43.4 %all_to_all.15 = f32[16,3,2,8,8,128]{5,4,2,1,0,3:T(8,128)} all-to-all(f32[16,3,2,8,8,128]{5,4,2,1,0,3:T(8,128)S(1)} %copy.19), channel_id=1, replica_groups=mesh['slab'=32,'snap'=8] {'snap'}, dimensions={3} | all-to-all | bytes 6291456 | tf_op jit(solution)/shard_map/all_to_all | solution.py:105
  86.2 2.8 reshape_squeeze.3
  89.0 3.2 %fusion.34 = f32[128,128]{1,0:T(8,128)} fusion(f32[128,6144]{1,0:T(8,128)S(1)} %reshape_squeeze.3), kind=kOutput, calls=%fused_computation.69 | convolution fusion | flops 1207959552 | bytes 3211264 | tf_op jit(solution)/shard_map/dot_general | solution.py:73
  92.2 0.2 all-reduce.5.cloned.1.call-start
  92.4 140.2 %all-reduce.3.cloned.1.call-done = f32[128,128]{1,0:T(8,128)} async-done(((f32[128,128]{1,0:T(8,128)}), f32[128,128]{1,0:T(8,128)}) %all-reduce.3.cloned.1.call-update) | async-done | bytes 65552 | tf_op jit(solution)/shard_map/psum | solution.py:108
  232.7 2.4 copy.16
  235.1 65.2 %all-reduce.5.cloned.1.call-done = f32[128,128]{1,0:T(8,128)} async-done(((f32[128,128]{1,0:T(8,128)}), f32[128,128]{1,0:T(8,128)}) %all-reduce.5.cloned.1.call-update) | async-done | bytes 65552 | tf_op jit(solution)/shard_map/psum | solution.py:108
  300.2 1.5 multiply_reduce_fusion
  302.4 1.0 fusion.6
  303.6 1.0 fusion.24
  304.7 0.2 fusion.5
  305.3 0.2 fusion.4
  306.6 0.2 fusion.2
  307.2 0.2 fusion.1
  307.7 3.0 fusion.43
  310.7 3.5 %copy.17 = f32[128,3,2,8,128]{4,3,2,1,0:T(8,128)} copy(f32[128,3,2,8,128]{4,0,3,2,1:T(8,128)S(1)} %fusion.43) | data formatting | bytes 6291456 | tf_op jit(solution)/shard_map/dot_general | solution.py:111
  (29 shorter events, 2.6 us)
Async XLA Ops:
  6.5 28.2 %copy-start = (bf16[16,3,2,64,128]{4,3,2,1,0:T(8,128)(2,1)S(1)}, bf16[16,3,2,64,128]{4,3,2,1,0:T(8,128)(2,1)}, u32[]{:S(2)}) copy-start(bf16[16,3,2,64,128]{4,3,2,1,0:T(8,128)(2,1)} %param.4) | copy-start | bytes 4718596
  6.5 28.2 %copy-start.2 = (bf16[3,2,64,128]{3,2,1,0:T(8,128)(2,1)S(1)}, bf16[3,2,64,128]{3,2,1,0:T(8,128)(2,1)}, u32[]{:S(2)}) copy-start(bf16[3,2,64,128]{3,2,1,0:T(8,128)(2,1)} %param.5) | copy-start | bytes 294916
  6.5 8.2 %copy-start.3 = (f32[128,64]{0,1:T(8,128)S(1)}, f32[128,64]{0,1:T(8,128)}, u32[]{:S(2)}) copy-start(f32[128,64]{0,1:T(8,128)} %param.6) | copy-start | bytes 98308
  6.5 226.1 %all-reduce.3.cloned.1.call-start = ((), (), s32[]{:S(2)}) async-start(), calls=%async_computation.1 | async-start | bytes 131072 | tf_op jit(solution)/shard_map/psum | solution.py:108
  9.4 21.6 %collective-permute-start = (bf16[17,3,1,64,128]{4,3,2,1,0:T(8,128)(2,1)}, bf16[17,3,1,64,128]{4,3,2,1,0:T(8,128)(2,1)S(1)}, u32[]{:S(2)}, u32[]{:S(2)}) collective-permute-start(bf16[17,3,1,64,128]{4,3,2,1,0:T(8,128)(2,1)} %get-tuple-element.20), channel_id=1, source_target_pairs={{0,8},{8,16},{16,24},{24,32},{32,40},{40,48},{48,56},{56,64},{64,7... | collective-permute-start | bytes 2506760 | tf_op jit(solution)/shard_map/ppermute | solution.py:14
  13.5 21.3 %collective-permute-start.1 = (bf16[17,3,1,64,128]{4,3,2,1,0:T(8,128)(2,1)}, bf16[17,3,1,64,128]{4,3,2,1,0:T(8,128)(2,1)S(1)}, u32[]{:S(2)}, u32[]{:S(2)}) collective-permute-start(bf16[17,3,1,64,128]{4,3,2,1,0:T(8,128)(2,1)} %get-tuple-element.21), channel_id=1, source_target_pairs={{8,0},{16,8},{24,16},{32,24},{40,32},{48,40},{56,48},{64,56},{72,6... | collective-permute-start | bytes 2506760 | tf_op jit(solution)/shard_map/ppermute | solution.py:17
  92.2 208.0 %all-reduce.5.cloned.1.call-start = ((), (), s32[]{:S(2)}) async-start(), calls=%async_computation.2 | async-start | bytes 131072 | tf_op jit(solution)/shard_map/psum | solution.py:108
  235.1 72.6 %copy-start.1 = (f32[6144,128]{1,0:T(8,128)S(1)}, f32[6144,128]{1,0:T(8,128)}, u32[]{:S(2)}) copy-start(f32[6144,128]{1,0:T(8,128)} %copy.16) | copy-start | bytes 9437188
Sparse Core Ops, SparseCore 0:
  92.3 140.2 all-reduce.2
  235.0 65.1 all-reduce.4
